TPU v7x, 512 devices: a whole 4x4x16 slice. The times are simulated.
512 devices in a mesh: row: 16 (over z), col: 32 (over y, x, core).
Axes of the slice: x: 4, y: 4, z: 16, core: 2. Of those that a mesh axis runs over, the one named last changes fastest.
Arguments:
- new_keys: bfloat16 [1024, 28672], P('col', 'row'), may hold values from -6 to 6
- precision: bfloat16 [28672, 28672], P('row', 'col'), may hold values from -0.03125 to 0.03125
- stored_keys: bfloat16 [32, 256, 28672], P('row', None, 'col'), may hold values from -0.03125 to 0.03125
- pair_batch: int32 [16, 24], replicated, may hold values from 0 to 31, as said below
- pair_count: int32 [16], replicated, may hold values from 8 to 24, as said below
- batch_length: int32 [32], replicated, may hold values from 64 to 256
- batch_slot: int32 [32], replicated, may hold values from 0 to 31, each once
Outputs:
- whitened: bfloat16 [1024, 28672], P('row', 'col')
- intersections: float32 [16, 24, 64, 256], P('row', None, 'col')
Inputs may be any that keep to these rules, and one draw needn't show every extreme that they name: `pair_batch`: the ids in one block's row are distinct; ids at places at or beyond the block's count are ignored. `pair_count`: some block lists exactly 24 batches. `batch_slot`: every store slot belongs to exactly one batch.
All inputs are finite; a program needn't handle non-finite values.
Results may differ from a plain program's by a relative error of at most 0.0029.
Values may be sent and summed in bfloat16 or wider, within the bound.
A program may use at most 64 MiB of HBM per device.

v0:
```python
import jax
import jax.numpy as jnp
from jax import lax
from jax.sharding import PartitionSpec as P


def shards(new_keys, precision, stored_keys, pair_batch, pair_count, batch_length, batch_slot):
    row_count = lax.axis_size("row")
    col_count = lax.axis_size("col")
    row_index = lax.axis_index("row")
    total_keys = new_keys.shape[0] * col_count
    block_keys = total_keys // row_count
    part_keys = block_keys // col_count
    local_batches, batch_keys, width = stored_keys.shape
    partial_value = jnp.dot(
        lax.all_gather(new_keys, "col", axis=0, tiled=True),
        precision,
        preferred_element_type=jnp.float32,
    )
    summed = lax.psum_scatter(partial_value, "row", scatter_dimension=0, tiled=True)
    whitened = summed.astype(jnp.bfloat16)
    every_row = lax.all_gather(whitened, "row", axis=0, tiled=True)
    rows = every_row.reshape(row_count, col_count, part_keys, width)
    terms = jnp.einsum("bcid,sjd->csbij", rows, stored_keys, preferred_element_type=jnp.float32)
    mine = lax.psum_scatter(terms, "col", scatter_dimension=0, tiled=True)[0]
    routed = lax.all_to_all(mine, "row", split_axis=1, concat_axis=0, tiled=True)
    table = routed[:, 0]
    listed = pair_batch[row_index]
    slots = batch_slot[listed]
    lengths = batch_length[listed]
    count = pair_count[row_index]
    picked = jnp.take(table, slots, axis=0)
    places = jnp.arange(slots.shape[0], dtype=jnp.int32)
    columns = jnp.arange(batch_keys, dtype=jnp.int32)
    keep = (places < count)[:, None, None] & (columns[None, None, :] < lengths[:, None, None])
    shares = jnp.where(keep, picked, jnp.zeros_like(picked))
    return (whitened, shares[None])


def solution(mesh):
    placed = (P("col", "row"), P("row", "col"), P("row", None, "col"), P(), P(), P(), P())
    return jax.shard_map(
        shards,
        mesh=mesh,
        in_specs=placed,
        out_specs=(P("row", "col"), P("row", None, "col", None)),
        check_vma=False,
    )
```

profile of v0, /device:TPU:6, one launch (start us, length us, event | category | flops | bytes accessed | tf_op | source)
XLA Modules:
  0.0 379.6 jit_solution(4652722605744629083)
XLA Ops:
  7.2 0.0 copy-start
  7.2 0.0 all-gather.3.cloned.1.call-start
  7.2 0.7 all-gather.3.cloned.1.call-update
  7.9 0.0 reduce-scatter.3.cloned.1.call-start
  8.0 68.1 %all-gather.3.cloned.1.call-done = bf16[1024,1792]{1,0:T(8,128)(2,1)} async-done(((bf16[32,1792]{1,0:T(8,128)(2,1)}), bf16[1024,1792]{1,0:T(8,128)(2,1)}) %all-gather.3.cloned.1.call-update) | async-done | bytes 3670032 | tf_op jit(solution)/shard_map/all_gather | solution.py:16
  76.0 7.8 %fusion.10 = f32[1024,896]{1,0:T(8,128)} fusion(bf16[1024,1792]{1,0:T(8,128)(2,1)} %all-gather.3.cloned.1.call-done, bf16[1792,896]{1,0:T(8,128)(2,1)S(1)} %copy-done), kind=kOutput, calls=%fused_computation.20 | convolution fusion | flops 3288334336 | bytes 10551296 | tf_op jit(solution)/shard_map/dot_general | solution.py:15
  83.8 0.0 reduce-scatter.3.cloned.1.call-update
  83.8 0.0 all-gather.5.cloned.1.call-start
  83.9 78.2 %reduce-scatter.3.cloned.1.call-done = f32[64,896]{1,0:T(8,128)} async-done(((f32[1024,896]{1,0:T(8,128)}), f32[64,896]{1,0:T(8,128)}) %reduce-scatter.3.cloned.1.call-update) | async-done | bytes 229392 | tf_op jit(solution)/shard_map/reduce_scatter | solution.py:20
  162.1 1.6 convert_element_type.3
  163.7 0.0 all-gather.5.cloned.1.call-update
  163.7 0.0 reduce-scatter.5.cloned.1.call-start
  163.8 72.0 %all-gather.5.cloned.1.call-done = bf16[1024,896]{1,0:T(8,128)(2,1)} async-done(((bf16[64,896]{1,0:T(8,128)(2,1)}), bf16[1024,896]{1,0:T(8,128)(2,1)}) %all-gather.5.cloned.1.call-update) | async-done | bytes 1835024 | tf_op jit(solution)/shard_map/all_gather | solution.py:22
  235.8 4.8 %reshape.105 = bf16[16,32,2,896]{3,2,1,0:T(2,128)(2,1)} reshape(bf16[1024,896]{1,0:T(8,128)(2,1)} %all-gather.5.cloned.1.call-done) | data formatting | bytes 3670016 | tf_op jit(solution)/shard_map/reshape | solution.py:23
  240.7 3.0 fusion.2
  243.7 0.0 copy-start.3
  243.7 0.0 copy-start.1
  243.7 0.0 copy-start.2
  243.7 2.5 copy.16
  246.2 0.0 reduce-scatter.5.cloned.1.call-update
  246.3 0.6 dynamic_slice.6
  246.9 0.7 fusion.8
  247.6 0.7 gather_fusion.1
  248.3 96.7 %reduce-scatter.5.cloned.1.call-done = f32[1,2,16,2,256]{4,2,3,1,0:T(8,128)} async-done(((f32[32,2,16,2,256]{4,2,3,1,0:T(8,128)}), f32[1,2,16,2,256]{4,2,3,1,0:T(8,128)}) %reduce-scatter.5.cloned.1.call-update) | async-done | bytes 65552 | tf_op jit(solution)/shard_map/reduce_scatter | solution.py:25
  345.1 1.5 copy.17
  346.6 12.3 %all-to-all-start = ((f32[2,16,2,256]{3,2,0,1:T(2,128)}), f32[2,16,2,256]{3,2,0,1:T(2,128)S(1)}, u32[]{:S(2)}, u32[]{:S(2)}) async-start(f32[2,16,2,256]{3,2,0,1:T(2,128)} %copy.17), calls=%async_computation.2 | async-start | bytes 131072 | tf_op jit(solution)/shard_map/all_to_all | solution.py:26
  358.9 0.7 iota_compare_fusion.1
  359.6 0.7 gather_fusion
  360.3 0.1 fusion.7
  360.4 11.4 %all-to-all-done = f32[2,16,2,256]{3,2,0,1:T(2,128)S(1)} async-done(((f32[2,16,2,256]{3,2,0,1:T(2,128)}), f32[2,16,2,256]{3,2,0,1:T(2,128)S(1)}, u32[]{:S(2)}, u32[]{:S(2)}) %all-to-all-start) | async-done | bytes 65568 | tf_op jit(solution)/shard_map/all_to_all | solution.py:26
  371.8 0.6 gather_fusion.2
  372.4 0.7 fusion.6
  (8 shorter events, 0.0 us)
Async XLA Ops:
  7.2 68.9 %copy-start = (bf16[1792,896]{1,0:T(8,128)(2,1)S(1)}, bf16[1792,896]{1,0:T(8,128)(2,1)}, u32[]{:S(2)}) copy-start(bf16[1792,896]{1,0:T(8,128)(2,1)} %param.8) | copy-start | bytes 9633796
  7.2 68.9 %all-gather.3.cloned.1.call-start = ((), (), s32[]{:S(2)}) async-start(), calls=%async_computation.3 | async-start | bytes 3784704 | tf_op jit(solution)/shard_map/all_gather | solution.py:16
  7.9 154.2 %reduce-scatter.3.cloned.1.call-start = ((), (), s32[]{:S(2)}) async-start(), calls=%async_computation.4 | async-start | bytes 3899392 | tf_op jit(solution)/shard_map/reduce_scatter | solution.py:20
  83.8 152.0 %all-gather.5.cloned.1.call-start = ((), (), s32[]{:S(2)}) async-start(), calls=%async_computation.5 | async-start | bytes 1949696 | tf_op jit(solution)/shard_map/all_gather | solution.py:22
  163.7 181.3 %reduce-scatter.5.cloned.1.call-start = ((), (), s32[]{:S(2)}) async-start(), calls=%async_computation.6 | async-start | bytes 2162688 | tf_op jit(solution)/shard_map/reduce_scatter | solution.py:25
  243.7 2.6 copy-start.3
  243.7 3.9 %copy-start.1 = (s32[32]{0:T(128)S(1)}, s32[32]{0:T(128)}, u32[]{:S(2)}) copy-start(s32[32]{0:T(128)} %param.13) | copy-start | bytes 388
  243.7 115.9 %copy-start.2 = (s32[32]{0:T(128)S(1)}, s32[32]{0:T(128)}, u32[]{:S(2)}) copy-start(s32[32]{0:T(128)} %param.12) | copy-start | bytes 388
  346.6 25.2 %all-to-all-start = ((f32[2,16,2,256]{3,2,0,1:T(2,128)}), f32[2,16,2,256]{3,2,0,1:T(2,128)S(1)}, u32[]{:S(2)}, u32[]{:S(2)}) async-start(f32[2,16,2,256]{3,2,0,1:T(2,128)} %copy.17), calls=%async_computation.2 | async-start | bytes 131072 | tf_op jit(solution)/shard_map/all_to_all | solution.py:26
Sparse Core Ops, SparseCore 0:
  11.1 64.8 all-gather.2
  84.0 78.1 reduce-scatter.2
  164.8 71.0 all-gather.4
  246.4 98.6 reduce-scatter.4
where the time goes:
time: 380 us
  waiting for transfers between devices  327 us (86%)
  between operations  13.9 us (4%)
  starting transfers between devices  12.5 us (3%)
  local copies, waits for them, and re-layouts  11.5 us (3%)
  matrix products  10.8 us (3%)
    reduce_scatter x1, waiting for transfers between devices, shards(): mine = lax.psum_scatter(terms, 'col', scatter_dimension=0, tiled=True)[0]  96.7 us
    reduce_scatter x1, waiting for transfers between devices, shards(): lax.psum_scatter(partial_value, 'row', scatter_dimension=0, tiled=True)  78.2 us
    all_gather x1, waiting for transfers between devices, shards(): every_row = lax.all_gather(whitened, 'row', axis=0, tiled=True)  72 us
    all_gather x1, waiting for transfers between devices, shards(): lax.all_gather(new_keys, 'col', axis=0, tiled=True)  68.1 us
    all_to_all x1, starting transfers between devices, shards(): lax.all_to_all(mine, 'row', split_axis=1, concat_axis=0, tiled=True)  12.3 us
    all_to_all x1, waiting for transfers between devices, shards(): lax.all_to_all(mine, 'row', split_axis=1, concat_axis=0, tiled=True)  11.4 us
    dot_general x1, matrix products, shards(): jnp.dot(lax.all_gather(new_keys, 'col', axis=0, tiled=True), precision, p...  7.77 us
  transfers between devices with their start and end apart: 5, of which 5 were waited for; matrix products, arithmetic and copies ran while one was open for 1% of the time, Pallas kernels for 0%

commit v1 on v0

--- a/solution.py
+++ b/solution.py
@@ -13,7 +13,9 @@
     part_keys = block_keys // col_count
     local_batches, batch_keys, width = stored_keys.shape
     partial_value = jnp.dot(
-        lax.all_gather(new_keys, "col", axis=0, tiled=True),
+        jnp.concatenate(
+            lax.all_to_all(jnp.stack([new_keys] * lax.axis_size("col")), "col", 0, 0), axis=0
+        ),
         precision,
         preferred_element_type=jnp.float32,
     )

time: 380 us -> 364 us (0.958)
  waiting for transfers between devices: 327 us -> 260 us
  blocking collectives: 0 us -> 51.7 us
    all_gather x1 -> x0, waiting for transfers between devices: 68.1 us -> none  [shards(): lax.all_gather(new_keys, 'col', axis=0, tiled=True)]
    all_to_all x0 -> x1, blocking collectives: none -> 51.7 us  [shards(): lax.all_to_all(jnp.stack([new_keys] * lax.axis_size('col')), 'col', 0, 0)]
  transfers between devices with their start and end apart: 5 -> 4, of which waited for: 5 -> 4; matrix products, arithmetic and copies ran while one was open for 1% -> 1% of each run, Pallas kernels for 0% -> 0%
where the time goes in v1:
time: 364 us
  waiting for transfers between devices  260 us (71%)
  blocking collectives  51.7 us (14%)
  between operations  13.8 us (4%)
  local copies, waits for them, and re-layouts  12.9 us (4%)
  starting transfers between devices  12.4 us (3%)
  matrix products  8.78 us (2%)
  other arithmetic  3.77 us (1%)
    reduce_scatter x1, waiting for transfers between devices, shards(): mine = lax.psum_scatter(terms, 'col', scatter_dimension=0, tiled=True)[0]  96.7 us
    reduce_scatter x1, waiting for transfers between devices, shards(): lax.psum_scatter(partial_value, 'row', scatter_dimension=0, tiled=True)  80.5 us
    all_gather x1, waiting for transfers between devices, shards(): every_row = lax.all_gather(whitened, 'row', axis=0, tiled=True)  71.4 us
    all_to_all x1, blocking collectives, shards(): lax.all_to_all(jnp.stack([new_keys] * lax.axis_size('col')), 'col', 0, 0)  51.7 us
    all_to_all x1, starting transfers between devices, shards(): lax.all_to_all(mine, 'row', split_axis=1, concat_axis=0, tiled=True)  12.3 us
    all_to_all x1, waiting for transfers between devices, shards(): lax.all_to_all(mine, 'row', split_axis=1, concat_axis=0, tiled=True)  11.4 us
  transfers between devices with their start and end apart: 4, of which 4 were waited for; matrix products, arithmetic and copies ran while one was open for 1% of the time, Pallas kernels for 0%

profile of v1, /device:TPU:6, one launch (start us, length us, event | category | flops | bytes accessed | tf_op | source)
XLA Modules:
  0.0 363.5 jit_solution(14834331706619527535)
XLA Ops:
  7.2 0.0 copy-start
  7.2 0.0 reduce-scatter.3.cloned.1.call-start
  7.2 1.5 stack.2
  8.7 51.7 %all_to_all.20 = bf16[32,32,1792]{2,1,0:T(8,128)(2,1)S(1)} all-to-all(bf16[32,32,1792]{2,1,0:T(8,128)(2,1)S(1)} %stack.2), channel_id=1, replica_groups=mesh['row'=16,'col'=32] {'col'}, dimensions={0} | all-to-all | bytes 7340032 | tf_op jit(solution)/shard_map/all_to_all | solution.py:17
  60.4 0.0 copy-done
  60.4 5.8 %fusion.10 = f32[1024,896]{1,0:T(8,128)} fusion(bf16[1024,1792]{1,0:T(8,128)(2,1)S(1)} %bitcast.30, bf16[1792,896]{1,0:T(8,128)(2,1)S(1)} %copy-done), kind=kOutput, calls=%fused_computation.20 | convolution fusion | flops 3288334336 | bytes 10551296 | tf_op jit(solution)/shard_map/dot_general | solution.py:15
  66.2 0.0 reduce-scatter.3.cloned.1.call-update
  66.2 0.0 all-gather.2.cloned.1.call-start
  66.2 80.5 %reduce-scatter.3.cloned.1.call-done = f32[64,896]{1,0:T(8,128)} async-done(((f32[1024,896]{1,0:T(8,128)}), f32[64,896]{1,0:T(8,128)}) %reduce-scatter.3.cloned.1.call-update) | async-done | bytes 229392 | tf_op jit(solution)/shard_map/reduce_scatter | solution.py:22
  146.7 1.6 convert_element_type.3
  148.3 0.0 all-gather.2.cloned.1.call-update
  148.3 0.0 reduce-scatter.5.cloned.1.call-start
  148.4 71.4 %all-gather.2.cloned.1.call-done = bf16[1024,896]{1,0:T(8,128)(2,1)} async-done(((bf16[64,896]{1,0:T(8,128)(2,1)}), bf16[1024,896]{1,0:T(8,128)(2,1)}) %all-gather.2.cloned.1.call-update) | async-done | bytes 1835024 | tf_op jit(solution)/shard_map/all_gather | solution.py:24
  219.8 4.8 %reshape.111 = bf16[16,32,2,896]{3,2,1,0:T(2,128)(2,1)} reshape(bf16[1024,896]{1,0:T(8,128)(2,1)} %all-gather.2.cloned.1.call-done) | data formatting | bytes 3670016 | tf_op jit(solution)/shard_map/reshape | solution.py:25
  224.5 3.0 fusion.2
  227.6 0.0 copy-start.3
  227.6 0.0 copy-start.1
  227.6 0.0 copy-start.2
  227.6 2.6 copy.16
  230.1 0.0 reduce-scatter.5.cloned.1.call-update
  230.2 0.6 dynamic_slice.6
  230.8 0.7 fusion.8
  231.5 0.7 gather_fusion.1
  232.2 96.7 %reduce-scatter.5.cloned.1.call-done = f32[1,2,16,2,256]{4,2,3,1,0:T(8,128)} async-done(((f32[32,2,16,2,256]{4,2,3,1,0:T(8,128)}), f32[1,2,16,2,256]{4,2,3,1,0:T(8,128)}) %reduce-scatter.5.cloned.1.call-update) | async-done | bytes 65552 | tf_op jit(solution)/shard_map/reduce_scatter | solution.py:27
  329.0 1.5 copy.17
  330.5 12.3 %all-to-all-start.1 = ((f32[2,16,2,256]{3,2,0,1:T(2,128)}), f32[2,16,2,256]{3,2,0,1:T(2,128)S(1)}, u32[]{:S(2)}, u32[]{:S(2)}) async-start(f32[2,16,2,256]{3,2,0,1:T(2,128)} %copy.17), calls=%async_computation.3 | async-start | bytes 131072 | tf_op jit(solution)/shard_map/all_to_all | solution.py:28
  342.8 0.7 iota_compare_fusion.1
  343.5 0.7 gather_fusion
  344.2 0.1 fusion.7
  344.2 11.4 %all-to-all-done.1 = f32[2,16,2,256]{3,2,0,1:T(2,128)S(1)} async-done(((f32[2,16,2,256]{3,2,0,1:T(2,128)}), f32[2,16,2,256]{3,2,0,1:T(2,128)S(1)}, u32[]{:S(2)}, u32[]{:S(2)}) %all-to-all-start.1) | async-done | bytes 65568 | tf_op jit(solution)/shard_map/all_to_all | solution.py:28
  355.7 0.6 gather_fusion.2
  356.3 0.7 fusion.6
  (7 shorter events, 0.0 us)
Async XLA Ops:
  7.2 53.2 %copy-start = (bf16[1792,896]{1,0:T(8,128)(2,1)S(1)}, bf16[1792,896]{1,0:T(8,128)(2,1)}, u32[]{:S(2)}) copy-start(bf16[1792,896]{1,0:T(8,128)(2,1)} %param.8) | copy-start | bytes 9633796
  7.2 139.5 %reduce-scatter.3.cloned.1.call-start = ((), (), s32[]{:S(2)}) async-start(), calls=%async_computation.4 | async-start | bytes 3899392 | tf_op jit(solution)/shard_map/reduce_scatter | solution.py:22
  66.2 153.6 %all-gather.2.cloned.1.call-start = ((), (), s32[]{:S(2)}) async-start(), calls=%async_computation.5 | async-start | bytes 1949696 | tf_op jit(solution)/shard_map/all_gather | solution.py:24
  148.3 180.6 %reduce-scatter.5.cloned.1.call-start = ((), (), s32[]{:S(2)}) async-start(), calls=%async_computation.6 | async-start | bytes 2162688 | tf_op jit(solution)/shard_map/reduce_scatter | solution.py:27
  227.6 2.6 copy-start.3
  227.6 3.9 %copy-start.1 = (s32[32]{0:T(128)S(1)}, s32[32]{0:T(128)}, u32[]{:S(2)}) copy-start(s32[32]{0:T(128)} %param.13) | copy-start | bytes 388
  227.6 115.9 %copy-start.2 = (s32[32]{0:T(128)S(1)}, s32[32]{0:T(128)}, u32[]{:S(2)}) copy-start(s32[32]{0:T(128)} %param.12) | copy-start | bytes 388
  330.5 25.2 %all-to-all-start.1 = ((f32[2,16,2,256]{3,2,0,1:T(2,128)}), f32[2,16,2,256]{3,2,0,1:T(2,128)S(1)}, u32[]{:S(2)}, u32[]{:S(2)}) async-start(f32[2,16,2,256]{3,2,0,1:T(2,128)} %copy.17), calls=%async_computation.3 | async-start | bytes 131072 | tf_op jit(solution)/shard_map/all_to_all | solution.py:28
Sparse Core Ops, SparseCore 0:
  66.3 80.3 reduce-scatter.2
  149.4 70.3 all-gather.1
  230.3 98.6 reduce-scatter.4
